TPU v7x, 512 devices: a whole 4x4x16 slice. The times are simulated.
512 devices in a mesh: grp: 8 (over x, core), path: 64 (over z, y).
Axes of the slice: x: 4, y: 4, z: 16, core: 2. Of those that a mesh axis runs over, the one named last changes fastest.
Arguments:
- normals: float32 [32, 8388608], P(None, ('grp', 'path')), may hold values from -10.1 to 10.1
- spot_today: float32 [32], replicated, may hold values from 0.5 to 2
- volatility: float32 [32], replicated, may hold values from 0.1 to 0.5
- weights: float32 [32], replicated, may hold values from 0.5 to 1.5
- cash_flows: float32 [8388608], P(('grp', 'path')), may hold values from -300 to 300
- exercise: int32 [8388608], P(('grp', 'path')), may hold values 0 or 1
Outputs:
- path_value: float32 [8388608], P(('grp', 'path'))
- state_cot: float32 [32, 8388608], P(None, ('grp', 'path'))
- flow_cot: float32 [8388608], P(('grp', 'path'))
- greeks: float32 [2, 32], replicated
All inputs are finite; a program needn't handle non-finite values. No bound on the sum of `exercise` on one device may be relied on, other than what follows from the above.
Results may differ from a plain program's by a relative error of at most 0.0003.
Values sent between devices are 32-bit elements; how exact they have to be, the bound alone decides.
A program may use at most 64 MiB of HBM per device.

v0:
```python
import math
import jax
import jax.numpy as jnp
from jax import lax
from jax.sharding import PartitionSpec as P

expiry_time = 0.5
root_time = math.sqrt(0.5)
inv_root_two = 1.0 / math.sqrt(2.0)
notional = 20.0
soft_width = 0.02


def path_state(normals, spot_today, volatility):
    return spot_today[:, None] * jnp.exp(
        volatility[:, None] * (root_time * normals) - 0.5 * expiry_time * volatility[:, None] ** 2
    )


def basis_rows(state, spot_today, volatility):
    scaled = (state / spot_today[:, None] - 1.0) / (volatility[:, None] * root_time)
    leading = jnp.ones_like(scaled[:1])
    squares = (scaled * scaled - 1.0) * inv_root_two
    neighbour = scaled * jnp.roll(scaled, -1, axis=0)
    bounded = jnp.tanh(scaled[:-1])
    return jnp.concatenate([leading, scaled, squares, neighbour, bounded], axis=0)


def payoff(state, spot_today, weights):
    basket = jnp.sum(weights[:, None] * state, axis=0) / jnp.sum(weights * spot_today)
    return notional * soft_width * jax.nn.softplus((basket - 1.0) / soft_width)


def chol_solve(factor, rhs):
    first = lax.linalg.triangular_solve(factor, rhs, left_side=True, lower=True)
    return lax.linalg.triangular_solve(factor, first, left_side=True, lower=True, transpose_a=True)


def per_device(normals, spot_today, volatility, weights, cash_flows, exercise):
    assets, local_paths = normals.shape
    features = 4 * assets
    block_width = math.gcd(local_paths, 1024)
    block_count = local_paths // block_width
    path_total = local_paths * lax.axis_size("grp") * lax.axis_size("path")
    highest = lax.Precision.HIGHEST
    contract_last = (((1,), (1,)), ((), ()))

    def block_inputs(block_index):
        block_start = block_index * block_width
        draw_block = lax.dynamic_slice_in_dim(normals, block_start, block_width, 1)
        flow_block = lax.dynamic_slice_in_dim(cash_flows, block_start, block_width, 0)
        taken_flag = lax.dynamic_slice_in_dim(exercise, block_start, block_width, 0).astype(
            jnp.float32
        )
        return (draw_block, flow_block, taken_flag)

    def gram_step(block_index, running):
        gram_acc, moment_acc = running
        draw_block, flow_block, taken_flag = block_inputs(block_index)
        basis_block = basis_rows(
            path_state(draw_block, spot_today, volatility), spot_today, volatility
        )
        gram_acc = gram_acc + lax.dot_general(
            basis_block,
            basis_block,
            contract_last,
            precision=highest,
            preferred_element_type=jnp.float32,
        )
        targets = jnp.stack([flow_block, 1.0 - taken_flag])
        moment_acc = moment_acc + lax.dot_general(
            targets,
            basis_block,
            contract_last,
            precision=highest,
            preferred_element_type=jnp.float32,
        )
        return (gram_acc, moment_acc)

    zero_gram = jnp.zeros((features, features), jnp.float32)
    zero_moment = jnp.zeros((2, features), jnp.float32)
    gram_acc, moment_acc = lax.fori_loop(0, block_count, gram_step, (zero_gram, zero_moment))
    gram_sum, moment_sum = lax.psum((gram_acc, moment_acc), ("grp", "path"))
    gram_mean = gram_sum / path_total
    moment_mean = moment_sum / path_total
    factor = jnp.linalg.cholesky(gram_mean)
    coefficients = chol_solve(factor, moment_mean.T)
    regression = coefficients[:, 0]
    multiplier = coefficients[:, 1]
    coef_rows = coefficients.T

    def adjoint_step(block_index, running):
        value_out, state_out, flow_out, greek_acc = running
        draw_block, flow_block, taken_flag = block_inputs(block_index)
        state, path_back = jax.vjp(
            lambda spot_level, spread: path_state(draw_block, spot_level, spread),
            spot_today,
            volatility,
        )
        (basis_block, reward), feature_back = jax.vjp(
            lambda current, spot_level, spread: (
                basis_rows(current, spot_level, spread),
                payoff(current, spot_level, weights),
            ),
            state,
            spot_today,
            volatility,
        )
        fitted = lax.dot_general(
            coef_rows,
            basis_block,
            (((1,), (0,)), ((), ())),
            precision=highest,
            preferred_element_type=jnp.float32,
        )
        continuation = fitted[0]
        lam_phi = fitted[1]
        value_block = taken_flag * reward + (1.0 - taken_flag) * continuation
        rows_bar = (
            multiplier[:, None] * (flow_block - continuation)[None, :]
            + regression[:, None] * (1.0 - taken_flag - lam_phi)[None, :]
        )
        state_bar, spot_bar, spread_bar = feature_back((rows_bar, taken_flag))
        spot_path, spread_path = path_back(state_bar)
        greek_acc = greek_acc + jnp.stack([spot_bar + spot_path, spread_bar + spread_path])
        block_start = block_index * block_width
        value_out = lax.dynamic_update_slice_in_dim(value_out, value_block, block_start, 0)
        state_out = lax.dynamic_update_slice_in_dim(state_out, state_bar, block_start, 1)
        flow_out = lax.dynamic_update_slice_in_dim(flow_out, lam_phi, block_start, 0)
        return (value_out, state_out, flow_out, greek_acc)

    start_outs = (
        jnp.zeros((local_paths,), jnp.float32),
        jnp.zeros((assets, local_paths), jnp.float32),
        jnp.zeros((local_paths,), jnp.float32),
        jnp.zeros((2, assets), jnp.float32),
    )
    path_value, state_cot, flow_cot, greek_acc = lax.fori_loop(
        0, block_count, adjoint_step, start_outs
    )
    greeks = lax.psum(greek_acc, ("grp", "path")) / path_total
    return (path_value, state_cot, flow_cot, greeks)


def solution(mesh):
    in_specs = (P(None, ("grp", "path")), P(), P(), P(), P(("grp", "path")), P(("grp", "path")))
    out_specs = (P(("grp", "path")), P(None, ("grp", "path")), P(("grp", "path")), P())
    return jax.shard_map(
        per_device, mesh=mesh, in_specs=in_specs, out_specs=out_specs, check_vma=False
    )
```

profile of v0, /device:TPU:1, one launch (start us, length us, event | category | flops | bytes accessed | tf_op | source)
XLA Modules:
  0.0 799.2 jit_solution(2905008628798093460)
XLA Ops:
  7.9 80.4 %while.42 = (s32[]{:T(128)}, f32[128,128]{1,0:T(8,128)S(1)}, f32[2,128]{1,0:T(2,128)S(1)}, f32[32]{0:T(128)}, f32[32,16384]{1,0:T(8,128)}, /*index=5*/f32[32]{0:...) while((s32[]{:T(128)}, f32[128,128]{1,0:T(8,128)S(1)}, ...), condition=%wide.region_1.2_spmd.clone, body=%wide.region_0.1_spmd.clone.sunk | while | flops 204870208 | bytes 3562582 | solution.py:82
  91.7 111.2 %psum.22 = f32[2,128]{1,0:T(2,128)S(1)} all-reduce(f32[2,128]{1,0:T(2,128)S(1)} %get-tuple-element.642), channel_id=1, replica_groups=mesh['grp'=8,'path'=64] {'grp','path'}, use_global_device_ids=true, to_apply=%region_5.6 | all-reduce | flops 256 | bytes 2048 | tf_op jit(solution)/shard_map/psum | solution.py:83
  202.9 340.4 %all-reduce.5.cloned.1.call-done = f32[128,128]{0,1:T(8,128)} async-done(((f32[128,128]{0,1:T(8,128)}), f32[128,128]{0,1:T(8,128)}) %all-reduce.5.cloned.1.call-update) | async-done | bytes 65552 | tf_op jit(solution)/shard_map/psum | solution.py:83
  545.1 11.7 %cholesky.15 = f32[128,128]{1,0:T(8,128)S(1)} custom-call(f32[128,128]{1,0:T(8,128)S(1)} %fusion.19), custom_call_target="Cholesky" | custom-call | tf_op jit(solution)/shard_map/jit(cholesky)/cholesky | solution.py:86
  558.1 9.8 %custom-call.8 = f32[1,128,128]{1,2,0:T(8,128)S(1)} custom-call(f32[1,128,128]{2,1,0:T(8,128)S(1)} %fusion.14), custom_call_target="InvertDiagBlocksLowerTriangular" | custom-call | tf_op jit(solution)/shard_map/triangular_solve | solution.py:36
  568.7 121.5 %while.43 = (s32[]{:T(128)}, f32[16384]{0:T(1024)S(1)}, f32[32,16384]{1,0:T(8,128)S(1)}, f32[16384]{0:T(1024)S(1)}, f32[2,32]{1,0:T(2,128)S(1)}, /*index=5*/s32[...) while((s32[]{:T(128)}, f32[16384]{0:T(1024)S(1)}, ...), condition=%wide.region_15.16_spmd.clone, body=%wide.region_7.15_spmd.clone.sunk | while | flops 5333607 | bytes 5730625 | solution.py:138
  571.3 2.0 multiply_reduce_fusion.8
  574.8 1.3 fusion.49
  578.9 2.0 multiply_reduce_fusion.8
  582.4 1.3 fusion.49
  586.5 2.0 multiply_reduce_fusion.8
  590.0 1.3 fusion.49
  594.1 2.0 multiply_reduce_fusion.8
  597.6 1.3 fusion.49
  601.7 2.0 multiply_reduce_fusion.8
  605.2 1.3 fusion.49
  609.3 2.0 multiply_reduce_fusion.8
  616.9 2.0 multiply_reduce_fusion.8
  620.4 1.3 fusion.49
  624.5 2.0 multiply_reduce_fusion.8
  632.1 2.0 multiply_reduce_fusion.8
  635.6 1.3 fusion.49
  639.7 2.0 multiply_reduce_fusion.8
  647.3 2.0 multiply_reduce_fusion.8
  654.9 2.0 multiply_reduce_fusion.8
  658.4 1.3 fusion.49
  662.5 2.0 multiply_reduce_fusion.8
  670.1 2.0 multiply_reduce_fusion.8
  673.6 1.3 fusion.49
  677.7 2.0 multiply_reduce_fusion.8
  685.2 2.0 multiply_reduce_fusion.8
  690.3 101.5 %psum.23 = f32[2,32]{1,0:T(2,128)S(1)} all-reduce(f32[2,32]{1,0:T(2,128)S(1)} %get-tuple-element.646), channel_id=1, replica_groups=mesh['grp'=8,'path'=64] {'grp','path'}, use_global_device_ids=true, to_apply=%region_16.17 | all-reduce | flops 64 | bytes 512 | tf_op jit(solution)/shard_map/psum | solution.py:141
  (552 shorter events, 150.8 us)
Async XLA Ops:
  7.2 536.1 %all-reduce.5.cloned.1.call-start = ((), (), s32[]{:S(2)}) async-start(), calls=%async_computation | async-start | bytes 131072 | tf_op jit(solution)/shard_map/psum | solution.py:83
  7.9 81.2 %copy-start.1 = (f32[32]{0:T(128)S(1)}, f32[32]{0:T(128)}, u32[]{:S(2)}) copy-start(f32[32]{0:T(128)} %param.13) | copy-start | bytes 388
  88.3 480.4 %copy-start.2 = (f32[32]{0:T(128)S(1)}, f32[32]{0:T(128)}, u32[]{:S(2)}) copy-start(f32[32]{0:T(128)} %get-tuple-element.1153) | copy-start | bytes 388
  88.3 480.4 %copy-start.5 = (f32[32]{0:T(128)S(1)}, f32[32]{0:T(128)}, u32[]{:S(2)}) copy-start(f32[32]{0:T(128)} %get-tuple-element.1154) | copy-start | bytes 388
  690.2 102.1 %copy-start = (f32[32,16384]{1,0:T(8,128)}, f32[32,16384]{1,0:T(8,128)S(1)}, u32[]{:S(2)}) copy-start(f32[32,16384]{1,0:T(8,128)S(1)} %get-tuple-element.638) | copy-start | bytes 6291460
  690.3 102.1 %copy-start.3 = (f32[16384]{0:T(1024)}, f32[16384]{0:T(1024)S(1)}, u32[]{:S(2)}) copy-start(f32[16384]{0:T(1024)S(1)} %get-tuple-element.639) | copy-start | bytes 196612
  690.3 102.1 %copy-start.4 = (f32[16384]{0:T(1024)}, f32[16384]{0:T(1024)S(1)}, u32[]{:S(2)}) copy-start(f32[16384]{0:T(1024)S(1)} %get-tuple-element.637) | copy-start | bytes 196612
Sparse Core Ops, SparseCore 0:
  89.2 454.0 all-reduce.4
where the time goes:
time: 803 us; the launch traced here: 799 us
  waiting for transfers between devices  340 us (42%)
  blocking collectives  213 us (27%)
  other arithmetic  151 us (19%)
  local copies, waits for them, and re-layouts  40.1 us (5%)
  matrix products  24.6 us (3%)
  between operations  15.5 us (2%)
  loops' own time  14.4 us (2%)
    psum x1, waiting for transfers between devices, per_device(): gram_sum, moment_sum = lax.psum((gram_acc, moment_acc), ('grp', 'path'))  340 us
    psum x1, blocking collectives, per_device(): gram_sum, moment_sum = lax.psum((gram_acc, moment_acc), ('grp', 'path'))  111 us
    psum x1, blocking collectives, per_device(): greeks = lax.psum(greek_acc, ('grp', 'path')) / path_total  101 us
    mul x32, other arithmetic, basis_rows(): squares = (scaled * scaled - 1.0) * inv_root_two  33.1 us
    reduce_sum x16, other arithmetic, payoff(): jnp.sum(weights[:, None] * state, axis=0) / jnp.sum(weights * spot_today)  31.9 us
    concatenate x32, local copies, waits for them, and re-layouts, basis_rows(): jnp.concatenate([leading, scaled, squares, neighbour, bounded], axis=0)  21.9 us
    reduce_sum x16, other arithmetic, path_state(): volatility[:, None] * (root_time * normals)  21.4 us
  transfers between devices with their start and end apart: 1, of which 1 were waited for; matrix products, arithmetic and copies ran while one was open for 0% of the time, Pallas kernels for 0%

commit v1 on v0

--- a/solution.py
+++ b/solution.py
@@ -3,6 +3,7 @@
 import jax.numpy as jnp
 from jax import lax
 from jax.sharding import PartitionSpec as P
+from jax.lax import psum
 
 expiry_time = 0.5
 root_time = math.sqrt(0.5)
@@ -80,7 +81,13 @@
     zero_gram = jnp.zeros((features, features), jnp.float32)
     zero_moment = jnp.zeros((2, features), jnp.float32)
     gram_acc, moment_acc = lax.fori_loop(0, block_count, gram_step, (zero_gram, zero_moment))
-    gram_sum, moment_sum = lax.psum((gram_acc, moment_acc), ("grp", "path"))
+
+    def lay_the_spot(frame_in):
+        for idx in ("grp", "path"):
+            frame_in = psum(frame_in, idx)
+        return frame_in
+
+    gram_sum, moment_sum = lay_the_spot((gram_acc, moment_acc))
     gram_mean = gram_sum / path_total
     moment_mean = moment_sum / path_total
     factor = jnp.linalg.cholesky(gram_mean)

time: 803 us -> 693 us (0.86)
  waiting for transfers between devices: 340 us -> 201 us
  blocking collectives: 213 us -> 242 us
    psum x1 -> x2, waiting for transfers between devices: 340 us -> 201 us  [lay_the_spot(): frame_in = psum(frame_in, idx)]
    psum x1 -> x2, blocking collectives: 111 us -> 131 us  [lay_the_spot(): frame_in = psum(frame_in, idx)]
    psum x1, blocking collectives: 101 us -> 111 us  [per_device(): greeks = lax.psum(greek_acc, ('grp', 'path')) / path_total]
  transfers between devices with their start and end apart: 1 -> 2, of which waited for: 1 -> 2; matrix products, arithmetic and copies ran while one was open for 0% -> 0% of each run, Pallas kernels for 0% -> 0%
where the time goes in v1:
time: 693 us; the launch traced here: 689 us
  blocking collectives  242 us (35%)
  waiting for transfers between devices  201 us (29%)
  other arithmetic  151 us (22%)
  local copies, waits for them, and re-layouts  40.1 us (6%)
  matrix products  24.6 us (4%)
  between operations  15.5 us (2%)
  loops' own time  14.4 us (2%)
    psum x2, waiting for transfers between devices, lay_the_spot(): frame_in = psum(frame_in, idx)  201 us
    psum x2, blocking collectives, lay_the_spot(): frame_in = psum(frame_in, idx)  131 us
    psum x1, blocking collectives, per_device(): greeks = lax.psum(greek_acc, ('grp', 'path')) / path_total  111 us
    mul x32, other arithmetic, basis_rows(): squares = (scaled * scaled - 1.0) * inv_root_two  33.1 us
    reduce_sum x16, other arithmetic, payoff(): jnp.sum(weights[:, None] * state, axis=0) / jnp.sum(weights * spot_today)  31.9 us
    concatenate x32, local copies, waits for them, and re-layouts, basis_rows(): jnp.concatenate([leading, scaled, squares, neighbour, bounded], axis=0)  21.9 us
    reduce_sum x16, other arithmetic, path_state(): volatility[:, None] * (root_time * normals)  21.4 us
  transfers between devices with their start and end apart: 2, of which 2 were waited for; matrix products, arithmetic and copies ran while one was open for 0% of the time, Pallas kernels for 0%

profile of v1, /device:TPU:1, one launch (start us, length us, event | category | flops | bytes accessed | tf_op | source)
XLA Modules:
  0.0 689.3 jit_solution(3964433449698811156)
XLA Ops:
  7.9 80.4 %while.42 = (s32[]{:T(128)}, f32[128,128]{1,0:T(8,128)S(1)}, f32[2,128]{1,0:T(2,128)S(1)}, f32[32]{0:T(128)}, f32[32,16384]{1,0:T(8,128)}, /*index=5*/f32[32]{0:...) while((s32[]{:T(128)}, f32[128,128]{1,0:T(8,128)S(1)}, ...), condition=%wide.region_1.2_spmd.clone, body=%wide.region_0.1_spmd.clone.sunk | while | flops 204870208 | bytes 3562582 | solution.py:83
  89.1 79.1 %all-reduce.6.cloned.1.call-done = f32[128,128]{0,1:T(8,128)} async-done(((f32[128,128]{0,1:T(8,128)}), f32[128,128]{0,1:T(8,128)}) %all-reduce.6.cloned.1.call-update) | async-done | bytes 65552 | tf_op jit(solution)/shard_map/psum | solution.py:87
  170.9 13.8 %psum.37 = f32[2,128]{1,0:T(2,128)S(1)} all-reduce(f32[2,128]{1,0:T(2,128)S(1)} %get-tuple-element.642), channel_id=1, replica_groups=mesh['grp'=8,'path'=64] {'grp'}, use_global_device_ids=true, to_apply=%region_6.7 | all-reduce | flops 256 | bytes 2048 | tf_op jit(solution)/shard_map/psum | solution.py:87
  184.7 116.9 %psum.38 = f32[2,128]{1,0:T(2,128)S(1)} all-reduce(f32[2,128]{1,0:T(2,128)S(1)} %psum.37), channel_id=1, replica_groups=mesh['grp'=8,'path'=64] {'path'}, use_global_device_ids=true, to_apply=%region_7.8 | all-reduce | flops 256 | bytes 2048 | tf_op jit(solution)/shard_map/psum | solution.py:87
  301.6 121.8 %all-reduce.8.cloned.1.call-done = f32[128,128]{0,1:T(8,128)} async-done(((f32[128,128]{0,1:T(8,128)}), f32[128,128]{0,1:T(8,128)}) %all-reduce.8.cloned.1.call-update) | async-done | bytes 65552 | tf_op jit(solution)/shard_map/psum | solution.py:87
  425.2 11.7 %cholesky.15 = f32[128,128]{1,0:T(8,128)S(1)} custom-call(f32[128,128]{1,0:T(8,128)S(1)} %fusion.19), custom_call_target="Cholesky" | custom-call | tf_op jit(solution)/shard_map/jit(cholesky)/cholesky | solution.py:93
  438.3 9.8 %custom-call.8 = f32[1,128,128]{1,2,0:T(8,128)S(1)} custom-call(f32[1,128,128]{2,1,0:T(8,128)S(1)} %fusion.14), custom_call_target="InvertDiagBlocksLowerTriangular" | custom-call | tf_op jit(solution)/shard_map/triangular_solve | solution.py:37
  448.8 121.5 %while.43 = (s32[]{:T(128)}, f32[16384]{0:T(1024)S(1)}, f32[32,16384]{1,0:T(8,128)S(1)}, f32[16384]{0:T(1024)S(1)}, f32[2,32]{1,0:T(2,128)S(1)}, /*index=5*/s32[...) while((s32[]{:T(128)}, f32[16384]{0:T(1024)S(1)}, ...), condition=%wide.region_17.18_spmd.clone, body=%wide.region_9.17_spmd.clone.sunk | while | flops 5333607 | bytes 5730625 | solution.py:145
  451.4 2.0 multiply_reduce_fusion.8
  454.9 1.3 fusion.49
  459.0 2.0 multiply_reduce_fusion.8
  462.5 1.3 fusion.49
  466.6 2.0 multiply_reduce_fusion.8
  470.1 1.3 fusion.49
  474.2 2.0 multiply_reduce_fusion.8
  481.8 2.0 multiply_reduce_fusion.8
  489.4 2.0 multiply_reduce_fusion.8
  497.0 2.0 multiply_reduce_fusion.8
  504.6 2.0 multiply_reduce_fusion.8
  508.1 1.3 fusion.49
  512.2 2.0 multiply_reduce_fusion.8
  519.8 2.0 multiply_reduce_fusion.8
  523.3 1.3 fusion.49
  527.4 2.0 multiply_reduce_fusion.8
  535.0 2.0 multiply_reduce_fusion.8
  542.6 2.0 multiply_reduce_fusion.8
  546.1 1.3 fusion.49
  550.2 2.0 multiply_reduce_fusion.8
  557.8 2.0 multiply_reduce_fusion.8
  561.3 1.3 fusion.49
  565.3 2.0 multiply_reduce_fusion.8
  570.4 111.5 %psum.39 = f32[2,32]{1,0:T(2,128)S(1)} all-reduce(f32[2,32]{1,0:T(2,128)S(1)} %get-tuple-element.646), channel_id=1, replica_groups=mesh['grp'=8,'path'=64] {'grp','path'}, use_global_device_ids=true, to_apply=%region_18.19 | all-reduce | flops 64 | bytes 512 | tf_op jit(solution)/shard_map/psum | solution.py:148
  (556 shorter events, 153.5 us)
Async XLA Ops:
  7.2 161.1 %all-reduce.6.cloned.1.call-start = ((), (), s32[]{:S(2)}) async-start(), calls=%async_computation | async-start | bytes 131072 | tf_op jit(solution)/shard_map/psum | solution.py:87
  7.9 160.4 %copy-start.1 = (f32[32]{0:T(128)S(1)}, f32[32]{0:T(128)}, u32[]{:S(2)}) copy-start(f32[32]{0:T(128)} %param.13) | copy-start | bytes 388
  88.3 360.5 %copy-start.2 = (f32[32]{0:T(128)S(1)}, f32[32]{0:T(128)}, u32[]{:S(2)}) copy-start(f32[32]{0:T(128)} %get-tuple-element.1154) | copy-start | bytes 388
  88.3 360.5 %copy-start.5 = (f32[32]{0:T(128)S(1)}, f32[32]{0:T(128)}, u32[]{:S(2)}) copy-start(f32[32]{0:T(128)} %get-tuple-element.1158) | copy-start | bytes 388
  89.1 334.3 %all-reduce.8.cloned.1.call-start = ((), (), s32[]{:S(2)}) async-start(), calls=%async_computation.1 | async-start | bytes 131072 | tf_op jit(solution)/shard_map/psum | solution.py:87
  570.3 112.1 %copy-start = (f32[32,16384]{1,0:T(8,128)}, f32[32,16384]{1,0:T(8,128)S(1)}, u32[]{:S(2)}) copy-start(f32[32,16384]{1,0:T(8,128)S(1)} %get-tuple-element.638) | copy-start | bytes 6291460
  570.4 112.1 %copy-start.3 = (f32[16384]{0:T(1024)}, f32[16384]{0:T(1024)S(1)}, u32[]{:S(2)}) copy-start(f32[16384]{0:T(1024)S(1)} %get-tuple-element.639) | copy-start | bytes 196612
  570.4 112.0 %copy-start.4 = (f32[16384]{0:T(1024)}, f32[16384]{0:T(1024)S(1)}, u32[]{:S(2)}) copy-start(f32[16384]{0:T(1024)S(1)} %get-tuple-element.637) | copy-start | bytes 196612
Sparse Core Ops, SparseCore 0:
  89.2 79.0 all-reduce.5
  171.7 251.6 all-reduce.7
